TPU v7x, 256 devices: a whole 4x4x8 slice. The times are simulated.
256 devices in a mesh: grp: 8 (over x, y_lo), wide: 32 (over y_hi, z, core).
Axes of the slice: x: 4, y: 4 (y_hi: 2, y_lo: 2; y = y_hi * 2 + y_lo), z: 8, core: 2. Of those that a mesh axis runs over, the one named last changes fastest.
Arguments:
- src_rows: float32 [262144, 400], P(('grp', 'wide')), may hold values from -16 to 16
- src_accum: float32 [262144], P(('grp', 'wide')), may hold values from 0.1 to 4
- dst_rows: float32 [16384, 400], P(('grp', 'wide')), may hold values from -1.5 to 1.5
- dst_accum: float32 [16384], P(('grp', 'wide')), may hold values from 0.1 to 4
- relations: float32 [1024, 400], replicated, may hold values from -4 to 4
- rel_ids: int32 [2, 262144], P(None, ('grp', 'wide')), may hold values from 0 to 1023
- targets: int32 [2, 262144], P(None, ('grp', 'wide')), may hold values from 0 to 2047
Outputs:
- new_src: float32 [262144, 400], P(('grp', 'wide'))
- new_src_accum: float32 [262144], P(('grp', 'wide'))
- new_dst: float32 [16384, 400], P(('grp', 'wide'))
- new_dst_accum: float32 [16384], P(('grp', 'wide'))
- edge_loss: float32 [2, 262144], P(None, ('grp', 'wide'))
All inputs are finite; a program needn't handle non-finite values.
Results may differ from a plain program's by a relative error of at most 0.009.
Values may be sent and summed in bfloat16 or wider, within the bound.
A program may use at most 64 MiB of HBM per device.

v0:
```python
import jax
import jax.numpy as jnp
from jax import lax
from jax.sharding import PartitionSpec as P

ROUNDS = 2
LEARN_RATE = 0.1


def passed_along(block, axis, distance):
    devices = range(lax.axis_size(axis))
    route = [((i - distance) % len(devices), i) for i in devices]
    return lax.ppermute(block, axis, route)


def adagrad(table_rows, accumulator, gradients):
    accumulator = accumulator + jnp.mean(gradients * gradients, axis=-1)
    return (table_rows - LEARN_RATE * gradients / jnp.sqrt(accumulator)[..., None], accumulator)


def score_blocks(key_rows, query_rows, label_ids):
    src_count, feat_width = query_rows.shape
    block_rows = 512
    block_count = src_count // block_rows

    def visit(running, pieces):
        query, labels = pieces
        logits = jnp.einsum("sd,bd->sb", query, key_rows, preferred_element_type=jnp.float32)
        top_score = jnp.max(logits, axis=1, keepdims=True)
        exp_scores = jnp.exp(logits - top_score)
        exp_total = jnp.sum(exp_scores, axis=1, keepdims=True)
        target_hit = lax.broadcasted_iota(jnp.int32, logits.shape, 1) == labels[:, None]
        picked = jnp.sum(jnp.where(target_hit, logits, 0.0), axis=1)
        losses = top_score[:, 0] + jnp.log(exp_total[:, 0]) - picked
        residual = (exp_scores / exp_total - target_hit.astype(jnp.float32)).astype(jnp.bfloat16)
        grad_query = jnp.dot(residual, key_rows, preferred_element_type=jnp.float32)
        running = running + jnp.einsum(
            "sb,sd->bd", residual, query, preferred_element_type=jnp.float32
        )
        return (running, (losses, grad_query))

    pieces = (
        query_rows.reshape(block_count, block_rows, feat_width),
        label_ids.reshape(block_count, block_rows),
    )
    zeros = jnp.zeros((key_rows.shape[0], feat_width), jnp.float32)
    running, outputs = lax.scan(visit, zeros, pieces)
    losses, grad_query = outputs
    return (losses.reshape(src_count), grad_query.reshape(src_count, feat_width), running)


def shards(src_rows, src_accum, dst_rows, dst_accum, relations, rel_ids, targets):
    loss_list = []
    for round_index in range(ROUNDS):
        key_rows = lax.all_gather(dst_rows.astype(jnp.bfloat16), "wide", axis=0, tiled=True)
        rel_scales = jnp.take(relations, rel_ids[round_index], axis=0)
        query_rows = (src_rows * rel_scales).astype(jnp.bfloat16)
        label_ids = targets[round_index]
        losses, grad_query, partial_value = score_blocks(key_rows, query_rows, label_ids)
        grad_dst = lax.psum_scatter(
            partial_value.astype(jnp.bfloat16), "wide", scatter_dimension=0, tiled=True
        ).astype(jnp.float32)
        src_rows, src_accum = adagrad(src_rows, src_accum, grad_query * rel_scales)
        dst_rows, dst_accum = adagrad(dst_rows, dst_accum, grad_dst)
        loss_list.append(losses)
        if round_index + 1 < ROUNDS:
            dst_rows, dst_accum = passed_along((dst_rows, dst_accum), "grp", 1)
    return (src_rows, src_accum, dst_rows, dst_accum, jnp.stack(loss_list))


def solution(mesh):
    placed = (
        P(("grp", "wide"), None),
        P(("grp", "wide")),
        P(("grp", "wide"), None),
        P(("grp", "wide")),
        P(),
        P(None, ("grp", "wide")),
        P(None, ("grp", "wide")),
    )
    return jax.shard_map(
        shards,
        mesh=mesh,
        in_specs=placed,
        out_specs=(
            P(("grp", "wide"), None),
            P(("grp", "wide")),
            P(("grp", "wide"), None),
            P(("grp", "wide")),
            P(None, ("grp", "wide")),
        ),
        check_vma=False,
    )
```

profile of v0, /device:TPU:2, one launch (start us, length us, event | category | flops | bytes accessed | tf_op | source)
XLA Modules:
  0.0 495.0 jit_solution(9824283437279981220)
XLA Ops:
  7.2 0.0 all-gather.3.cloned.1.call-start
  7.2 1.5 convert_element_type.37
  8.8 0.0 reduce-scatter.7.cloned.1.call-start
  8.8 1.8 copy.31
  10.7 2.8 copy.34
  13.6 4.9 gather_fusion
  18.5 2.5 multiply_convert_fusion.1
  21.0 73.1 %all-gather.3.cloned.1.call-done = bf16[2048,400]{1,0:T(8,128)(2,1)} async-done(((bf16[64,400]{1,0:T(8,128)(2,1)}), bf16[2048,400]{1,0:T(8,128)(2,1)}) %all-gather.3.cloned.1.call-update) | async-done | bytes 1638416 | tf_op jit(solution)/shard_map/all_gather | solution.py:55
  94.2 1.4 broadcast.38.clone
  95.5 31.9 %while.30 = (s32[]{:T(128)}, f32[2048,400]{0,1:T(8,128)}, f32[2,512]{1,0:T(2,128)S(1)}, f32[2,512,400]{1,2,0:T(8,128)}, bf16[2,512,400]{2,1,0:T(8,128)(2,1)S(1)}...) while((s32[]{:T(128)}, f32[2048,400]{0,1:T(8,128)}, ...), condition=%wide.region_4.6_spmd.clone, body=%wide.region_0.5_spmd.clone.sunk | while | flops 2530803200 | bytes 31064192 | solution.py:47
  95.5 3.0 fusion.60
  98.5 1.4 select_reduce_fusion.4
  99.9 2.5 subtract_convert_fusion.4
  102.4 4.3 select_add_fusion.4
  106.8 4.2 fusion.61
  111.0 3.0 fusion.60
  114.0 1.4 select_reduce_fusion.4
  115.4 2.5 subtract_convert_fusion.4
  117.9 5.3 %select_add_fusion.4 = f32[2048,400]{0,1:T(8,128)} fusion(f32[2048,400]{0,1:T(8,128)} %get-tuple-element.322, bf16[512,2048]{1,0:T(8,128)(2,1)} %subtract_convert_fusion.4, pred[]{:T(512)S(6)} %compare.6, bf16[2,512,400]{2,1,0:T(8,128)(2,1)S(1)} %get-tuple-element.334, s32[]{:T(128)S(6)} %copy.55), kind=kOutput, calls=%fused_computation.7.clone.1 | convolution fusion | flops 840499200 | bytes 9175045 | tf_op jit(solution)/shard_map/while/body/eval_jaxpr/sb,sd->bd/dot_general | solution.py:37
  123.3 4.2 fusion.61
  127.4 3.4 convert_element_type.39
  130.9 3.8 copy.41
  134.7 0.0 all-gather.5.cloned.1.call-start
  134.8 0.1 copy.36
  134.9 116.2 %reduce-scatter.7.cloned.1.call-done = bf16[64,400]{1,0:T(8,128)(2,1)} async-done(((bf16[2048,400]{1,0:T(8,128)(2,1)}), bf16[64,400]{1,0:T(8,128)(2,1)}) %reduce-scatter.7.cloned.1.call-update) | async-done | bytes 51216
  251.1 1.0 copy.42
  252.1 0.1 fusion.20
  252.2 0.7 collective-permute-start
  252.9 6.1 %collective-permute-done = f32[64,400]{0,1:T(8,128)S(1)} collective-permute-done((f32[64,400]{0,1:T(8,128)S(1)}, f32[64,400]{0,1:T(8,128)S(1)}, u32[]{:S(2)}, u32[]{:S(2)}) %collective-permute-start) | collective-permute-done | bytes 102432 | tf_op jit(solution)/shard_map/ppermute | solution.py:13
  258.9 0.7 copy.37
  259.7 0.2 reduce-scatter.9.cloned.1.call-start
  259.9 4.9 gather_fusion.1
  264.9 3.0 copy.33
  268.0 2.2 multiply_reduce_fusion.1
  270.2 0.6 copy-done.3
  270.9 3.3 multiply_convert_fusion
  274.1 63.0 %all-gather.5.cloned.1.call-done = bf16[2048,400]{1,0:T(8,128)(2,1)} async-done(((bf16[64,400]{1,0:T(8,128)(2,1)}), bf16[2048,400]{1,0:T(8,128)(2,1)}) %all-gather.5.cloned.1.call-update) | async-done | bytes 1638416 | tf_op jit(solution)/shard_map/all_gather | solution.py:55
  337.1 1.4 broadcast.38
  338.5 26.5 %while.31 = (s32[]{:T(128)}, f32[2048,400]{0,1:T(8,128)}, f32[2,512]{1,0:T(2,128)S(1)}, f32[2,512,400]{1,2,0:T(8,128)}, bf16[2,512,400]{2,1,0:T(8,128)(2,1)S(1)}...) while((s32[]{:T(128)}, f32[2048,400]{0,1:T(8,128)}, ...), condition=%wide.region_12.14_spmd.clone, body=%wide.region_8.13_spmd.clone.sunk | while | flops 2530803200 | bytes 31064192 | solution.py:47
  338.5 3.0 fusion.67
  341.5 1.4 select_reduce_fusion.5
  342.9 1.6 subtract_convert_fusion.5
  344.5 2.8 select_add_fusion.5
  347.3 3.5 fusion.68
  350.8 3.0 fusion.67
  353.8 1.4 select_reduce_fusion.5
  355.2 1.6 subtract_convert_fusion.5
  356.8 4.7 select_add_fusion.5
  361.5 3.5 fusion.68
  365.0 2.2 convert_element_type.42
  367.2 2.4 copy.43
  369.7 0.7 collective-permute-start.1
  370.3 2.9 copy.38
  373.2 2.2 multiply_reduce_fusion
  375.4 0.6 fusion.28
  376.1 0.0 copy-done.5
  376.1 1.8 divide_subtract_fusion
  377.9 2.8 copy.39
  380.7 0.6 pad_maximum_fusion
  381.3 104.8 %reduce-scatter.9.cloned.1.call-done = bf16[64,400]{1,0:T(8,128)(2,1)} async-done(((bf16[2048,400]{1,0:T(8,128)(2,1)}), bf16[64,400]{1,0:T(8,128)(2,1)}) %reduce-scatter.9.cloned.1.call-update) | async-done | bytes 51216
  486.1 1.0 copy.44
  487.1 0.1 fusion.23
  487.1 0.5 fusion.27
  487.7 0.8 copy.40
  (55 shorter events, 0.5 us)
Async XLA Ops:
  7.2 87.0 %all-gather.3.cloned.1.call-start = ((), (), s32[]{:S(2)}) async-start(), calls=%async_computation.2 | async-start | bytes 2162688 | tf_op jit(solution)/shard_map/all_gather | solution.py:55
  8.8 242.3 %reduce-scatter.7.cloned.1.call-start = ((), (), s32[]{:S(2)}) async-start(), calls=%async_computation.4 | async-start | bytes 2162688
  10.7 2.9 copy-start.8
  10.7 2.9 copy-start.9
  130.9 3.9 copy-start.6
  134.7 117.5 %copy-start.10 = (f32[64]{0:T(128)S(1)}, f32[64]{0:T(128)}, u32[]{:S(2)}) copy-start(f32[64]{0:T(128)} %param.16) | copy-start | bytes 772
  134.7 202.4 %all-gather.5.cloned.1.call-start = ((), (), s32[]{:S(2)}) async-start(), calls=%async_computation.3 | async-start | bytes 2162688 | tf_op jit(solution)/shard_map/all_gather | solution.py:55
  252.2 6.7 %collective-permute-start = (f32[64,400]{0,1:T(8,128)S(1)}, f32[64,400]{0,1:T(8,128)S(1)}, u32[]{:S(2)}, u32[]{:S(2)}) collective-permute-start(f32[64,400]{0,1:T(8,128)S(1)} %fusion.19), channel_id=1, source_target_pairs={{224,0},{0,32},{32,64},{64,96},{96,128},{128,160},{160,192},{192,2... | collective-permute-start | bytes 307208 | tf_op jit(solution)/shard_map/ppermute | solution.py:13
  259.7 226.4 %reduce-scatter.9.cloned.1.call-start = ((), (), s32[]{:S(2)}) async-start(), calls=%async_computation.5 | async-start | bytes 2162688
  264.9 3.1 copy-start
  267.9 2.3 copy-start.7
  267.9 2.3 copy-start.1
  267.9 2.9 copy-start.3
  369.7 3.5 copy-start.2
  369.7 117.4 %collective-permute-start.1 = (f32[64]{0:T(128)S(1)}, f32[64]{0:T(128)S(1)}, u32[]{:S(2)}, u32[]{:S(2)}) collective-permute-start(f32[64]{0:T(128)S(1)} %get-tuple-element.199), channel_id=1, source_target_pairs={{224,0},{0,32},{32,64},{64,96},{96,128},{128,160},{160,192},{192,2... | collective-permute-start | bytes 776 | tf_op jit(solution)/shard_map/ppermute | solution.py:13
  373.2 2.8 copy-start.4
  373.2 2.9 copy-start.5
Sparse Core Ops, SparseCore 0:
  11.3 82.7 all-gather.2
  134.8 116.2 reduce-scatter.6
  259.8 77.2 all-gather.4
  369.8 116.2 reduce-scatter.8
where the time goes:
time: 496 us; the launch traced here: 495 us
  waiting for transfers between devices  363 us (73%)
  matrix products  44.4 us (9%)
  local copies, waits for them, and re-layouts  36.6 us (7%)
  other arithmetic  35 us (7%)
  between operations  14 us (3%)
    unnamed x6, waiting for transfers between devices  221 us
    all_gather x2, waiting for transfers between devices, shards(): lax.all_gather(dst_rows.astype(jnp.bfloat16), 'wide', axis=0, tiled=True)  136 us
    unnamed x33, local copies, waits for them, and re-layouts  17.2 us
    dot_general x4, matrix products, visit(): jnp.einsum('sb,sd->bd', residual, query, preferred_element_type=jnp.float32)  17.1 us
    dot_general x4, matrix products, visit(): grad_query = jnp.dot(residual, key_rows, preferred_element_type=jnp.float32)  15.5 us
    dot_general x4, matrix products, visit(): jnp.einsum('sd,bd->sb', query, key_rows, preferred_element_type=jnp.float32)  11.8 us
  transfers between devices with their start and end apart: 6, of which 5 were waited for; matrix products, arithmetic and copies ran while one was open for 8% of the time, Pallas kernels for 0%

commit v1 on v0

--- a/solution.py
+++ b/solution.py
@@ -52,7 +52,9 @@
 def shards(src_rows, src_accum, dst_rows, dst_accum, relations, rel_ids, targets):
     loss_list = []
     for round_index in range(ROUNDS):
-        key_rows = lax.all_gather(dst_rows.astype(jnp.bfloat16), "wide", axis=0, tiled=True)
+        block_2 = dst_rows.astype(jnp.bfloat16)
+        stack = jnp.stack([block_2] * lax.axis_size("wide"))
+        key_rows = jnp.concatenate(lax.all_to_all(stack, "wide", 0, 0), axis=0)
         rel_scales = jnp.take(relations, rel_ids[round_index], axis=0)
         query_rows = (src_rows * rel_scales).astype(jnp.bfloat16)
         label_ids = targets[round_index]

time: 496 us -> 456 us (0.919)
  waiting for transfers between devices: 363 us -> 303 us
  starting transfers between devices: 1.67 us -> 19.4 us
    all_gather x2 -> x0, waiting for transfers between devices: 136 us -> none  [shards(): lax.all_gather(dst_rows.astype(jnp.bfloat16), 'wide', axis=0, tiled=True)]
    all_to_all x0 -> x2, waiting for transfers between devices: none -> 77.1 us  [shards(): key_rows = jnp.concatenate(lax.all_to_all(stack, 'wide', 0, 0), axis=0)]
    all_to_all x0 -> x2, starting transfers between devices: none -> 17.8 us  [shards(): key_rows = jnp.concatenate(lax.all_to_all(stack, 'wide', 0, 0), axis=0)]
    unnamed x6 -> x4, waiting for transfers between devices: 221 us -> 220 us
where the time goes in v1:
time: 456 us; the launch traced here: 455 us
  waiting for transfers between devices  303 us (66%)
  matrix products  44.4 us (10%)
  local copies, waits for them, and re-layouts  39.1 us (9%)
  other arithmetic  34.3 us (8%)
  starting transfers between devices  19.4 us (4%)
  between operations  14.3 us (3%)
    unnamed x4, waiting for transfers between devices  220 us
    all_to_all x2, waiting for transfers between devices, shards(): key_rows = jnp.concatenate(lax.all_to_all(stack, 'wide', 0, 0), axis=0)  77.1 us
    all_to_all x2, starting transfers between devices, shards(): key_rows = jnp.concatenate(lax.all_to_all(stack, 'wide', 0, 0), axis=0)  17.8 us
    unnamed x33, local copies, waits for them, and re-layouts  17.2 us
    dot_general x4, matrix products, visit(): jnp.einsum('sb,sd->bd', residual, query, preferred_element_type=jnp.float32)  17.1 us
    dot_general x4, matrix products, visit(): grad_query = jnp.dot(residual, key_rows, preferred_element_type=jnp.float32)  15.5 us
    dot_general x4, matrix products, visit(): jnp.einsum('sd,bd->sb', query, key_rows, preferred_element_type=jnp.float32)  11.8 us
    gather x2, local copies, waits for them, and re-layouts, shards(): rel_scales = jnp.take(relations, rel_ids[round_index], axis=0)  9.8 us
  transfers between devices with their start and end apart: 6, of which 5 were waited for; matrix products, arithmetic and copies ran while one was open for 8% of the time, Pallas kernels for 0%

profile of v1, /device:TPU:2, one launch (start us, length us, event | category | flops | bytes accessed | tf_op | source)
XLA Modules:
  0.0 455.0 jit_solution(15477853959088115230)
XLA Ops:
  7.2 0.9 convert_element_type.37
  8.1 1.6 stack.6
  9.6 11.6 %all-to-all-start = ((bf16[32,64,400]{2,1,0:T(8,128)(2,1)}), bf16[32,64,400]{2,1,0:T(8,128)(2,1)}, u32[]{:S(2)}, u32[]{:S(2)}) async-start(bf16[32,64,400]{2,1,0:T(8,128)(2,1)} %stack.6), calls=%async_computation | async-start | bytes 4194304 | tf_op jit(solution)/shard_map/all_to_all | solution.py:57
  21.3 1.8 copy.31
  23.2 2.8 copy.34
  26.1 4.9 %gather_fusion = f32[1024,400]{1,0:T(8,128)} fusion(f32[1024,400]{1,0:T(8,128)S(1)} %copy.31, s32[1024]{0:T(1024)S(1)} %fusion.24), kind=kCustom, calls=%fused_computation.clone | custom fusion | bytes 3280896 | tf_op jit(solution)/shard_map/jit(_take)/gather | solution.py:58
  31.0 2.5 multiply_convert_fusion.1
  33.5 39.6 %all-to-all-done = bf16[32,64,400]{2,1,0:T(8,128)(2,1)} async-done(((bf16[32,64,400]{2,1,0:T(8,128)(2,1)}), bf16[32,64,400]{2,1,0:T(8,128)(2,1)}, u32[]{:S(2)}, u32[]{:S(2)}) %all-to-all-start) | async-done | bytes 1638432 | tf_op jit(solution)/shard_map/all_to_all | solution.py:57
  73.1 1.4 broadcast.42.clone
  74.5 31.9 %while.30 = (s32[]{:T(128)}, f32[2048,400]{0,1:T(8,128)}, f32[2,512]{1,0:T(2,128)S(1)}, f32[2,512,400]{1,2,0:T(8,128)}, bf16[2,512,400]{2,1,0:T(8,128)(2,1)S(1)}...) while((s32[]{:T(128)}, f32[2048,400]{0,1:T(8,128)}, ...), condition=%wide.region_4.6_spmd.clone, body=%wide.region_0.5_spmd.clone.sunk | while | flops 2530803200 | bytes 31064192 | solution.py:47
  74.5 3.0 fusion.60
  77.4 1.4 select_reduce_fusion.4
  78.9 2.5 subtract_convert_fusion.4
  81.4 4.4 select_add_fusion.4
  85.8 4.2 fusion.61
  90.0 3.0 fusion.60
  92.9 1.4 select_reduce_fusion.4
  94.3 2.5 subtract_convert_fusion.4
  96.9 5.3 %select_add_fusion.4 = f32[2048,400]{0,1:T(8,128)} fusion(f32[2048,400]{0,1:T(8,128)} %get-tuple-element.315, bf16[512,2048]{1,0:T(8,128)(2,1)} %subtract_convert_fusion.4, pred[]{:T(512)S(6)} %compare.6, bf16[2,512,400]{2,1,0:T(8,128)(2,1)S(1)} %get-tuple-element.327, s32[]{:T(128)S(6)} %copy.55), kind=kOutput, calls=%fused_computation.7.clone.1 | convolution fusion | flops 840499200 | bytes 9175045 | tf_op jit(solution)/shard_map/while/body/eval_jaxpr/sb,sd->bd/dot_general | solution.py:37
  102.2 4.2 fusion.61
  106.4 3.4 convert_element_type.39
  109.8 3.8 copy.41
  113.7 0.1 copy.36
  113.8 116.0 %reduce-scatter.7.cloned.1.call-done = bf16[64,400]{1,0:T(8,128)(2,1)} async-done(((bf16[2048,400]{1,0:T(8,128)(2,1)}), bf16[64,400]{1,0:T(8,128)(2,1)}) %reduce-scatter.7.cloned.1.call-update) | async-done | bytes 51216
  229.8 1.0 copy.42
  230.7 0.1 fusion.20
  230.9 0.7 collective-permute-start
  231.6 6.0 %collective-permute-done = f32[64,400]{0,1:T(8,128)S(1)} collective-permute-done((f32[64,400]{0,1:T(8,128)S(1)}, f32[64,400]{0,1:T(8,128)S(1)}, u32[]{:S(2)}, u32[]{:S(2)}) %collective-permute-start) | collective-permute-done | bytes 102432 | tf_op jit(solution)/shard_map/ppermute | solution.py:13
  237.6 0.1 copy.37
  237.7 1.7 stack.7
  239.4 6.1 %all-to-all-start.1 = ((bf16[32,64,400]{2,1,0:T(8,128)(2,1)}), bf16[32,64,400]{2,1,0:T(8,128)(2,1)}, u32[]{:S(2)}, u32[]{:S(2)}) async-start(bf16[32,64,400]{2,1,0:T(8,128)(2,1)} %stack.7), calls=%async_computation.1 | async-start | bytes 4194304 | tf_op jit(solution)/shard_map/all_to_all | solution.py:57
  245.5 0.2 reduce-scatter.9.cloned.1.call-start
  245.8 4.9 %gather_fusion.1 = f32[1024,400]{1,0:T(8,128)} fusion(f32[1024,400]{1,0:T(8,128)S(1)} %copy.31, s32[1024]{0:T(1024)S(1)} %fusion.25), kind=kCustom, calls=%fused_computation.1.clone | custom fusion | bytes 3280896 | tf_op jit(solution)/shard_map/jit(_take)/gather | solution.py:58
  250.7 3.0 copy.33
  253.7 2.2 multiply_reduce_fusion.1
  256.0 0.6 copy-done.3
  256.5 3.3 multiply_convert_fusion
  259.8 37.5 %all-to-all-done.1 = bf16[32,64,400]{2,1,0:T(8,128)(2,1)} async-done(((bf16[32,64,400]{2,1,0:T(8,128)(2,1)}), bf16[32,64,400]{2,1,0:T(8,128)(2,1)}, u32[]{:S(2)}, u32[]{:S(2)}) %all-to-all-start.1) | async-done | bytes 1638432 | tf_op jit(solution)/shard_map/all_to_all | solution.py:57
  297.4 1.4 broadcast.42
  298.7 26.5 %while.31 = (s32[]{:T(128)}, f32[2048,400]{0,1:T(8,128)}, f32[2,512]{1,0:T(2,128)S(1)}, f32[2,512,400]{1,2,0:T(8,128)}, bf16[2,512,400]{2,1,0:T(8,128)(2,1)S(1)}...) while((s32[]{:T(128)}, f32[2048,400]{0,1:T(8,128)}, ...), condition=%wide.region_12.14_spmd.clone, body=%wide.region_8.13_spmd.clone.sunk | while | flops 2530803200 | bytes 31064192 | solution.py:47
  298.7 3.0 fusion.67
  301.7 1.4 select_reduce_fusion.5
  303.1 1.6 subtract_convert_fusion.5
  304.7 2.8 select_add_fusion.5
  307.5 3.5 fusion.68
  311.0 3.0 fusion.67
  314.0 1.4 select_reduce_fusion.5
  315.4 1.6 subtract_convert_fusion.5
  317.0 4.7 %select_add_fusion.5 = f32[2048,400]{0,1:T(8,128)} fusion(f32[2048,400]{0,1:T(8,128)} %get-tuple-element.342, bf16[512,2048]{1,0:T(8,128)(2,1)S(1)} %subtract_convert_fusion.5, pred[]{:T(512)S(6)} %compare.7, bf16[2,512,400]{2,1,0:T(8,128)(2,1)S(1)} %get-tuple-element.354, s32[]{:T(128)S(6)} %copy.67), kind=kOutput, calls=%fused_computation.24.clone.1 | convolution fusion | flops 840499200 | bytes 9175045 | tf_op jit(solution)/shard_map/while/body/eval_jaxpr/sb,sd->bd/dot_general | solution.py:37
  321.7 3.5 fusion.68
  325.3 2.2 convert_element_type.42
  327.4 2.4 copy.43
  329.9 0.6 collective-permute-start.1
  330.5 2.9 copy.38
  333.4 2.2 multiply_reduce_fusion
  335.6 0.6 fusion.28
  336.2 1.8 divide_subtract_fusion
  338.1 2.8 copy.39
  340.8 0.6 pad_maximum_fusion
  341.4 104.3 %reduce-scatter.9.cloned.1.call-done = bf16[64,400]{1,0:T(8,128)(2,1)} async-done(((bf16[2048,400]{1,0:T(8,128)(2,1)}), bf16[64,400]{1,0:T(8,128)(2,1)}) %reduce-scatter.9.cloned.1.call-update) | async-done | bytes 51216
  445.8 1.0 copy.44
  446.7 0.1 fusion.23
  446.8 0.5 fusion.27
  447.4 0.8 copy.40
  (55 shorter events, 0.5 us)
Async XLA Ops:
  9.6 63.5 %all-to-all-start = ((bf16[32,64,400]{2,1,0:T(8,128)(2,1)}), bf16[32,64,400]{2,1,0:T(8,128)(2,1)}, u32[]{:S(2)}, u32[]{:S(2)}) async-start(bf16[32,64,400]{2,1,0:T(8,128)(2,1)} %stack.6), calls=%async_computation | async-start | bytes 4194304 | tf_op jit(solution)/shard_map/all_to_all | solution.py:57
  21.3 208.5 %reduce-scatter.7.cloned.1.call-start = ((), (), s32[]{:S(2)}) async-start(), calls=%async_computation.4 | async-start | bytes 2162688
  23.2 2.9 copy-start.8
  23.2 2.9 copy-start.9
  109.8 3.8 copy-start.6
  113.6 117.2 %copy-start.10 = (f32[64]{0:T(128)S(1)}, f32[64]{0:T(128)}, u32[]{:S(2)}) copy-start(f32[64]{0:T(128)} %param.16) | copy-start | bytes 772
  230.9 6.7 %collective-permute-start = (f32[64,400]{0,1:T(8,128)S(1)}, f32[64,400]{0,1:T(8,128)S(1)}, u32[]{:S(2)}, u32[]{:S(2)}) collective-permute-start(f32[64,400]{0,1:T(8,128)S(1)} %fusion.19), channel_id=1, source_target_pairs={{224,0},{0,32},{32,64},{64,96},{96,128},{128,160},{160,192},{192,2... | collective-permute-start | bytes 307208 | tf_op jit(solution)/shard_map/ppermute | solution.py:13
  239.4 58.0 %all-to-all-start.1 = ((bf16[32,64,400]{2,1,0:T(8,128)(2,1)}), bf16[32,64,400]{2,1,0:T(8,128)(2,1)}, u32[]{:S(2)}, u32[]{:S(2)}) async-start(bf16[32,64,400]{2,1,0:T(8,128)(2,1)} %stack.7), calls=%async_computation.1 | async-start | bytes 4194304 | tf_op jit(solution)/shard_map/all_to_all | solution.py:57
  245.5 200.3 %reduce-scatter.9.cloned.1.call-start = ((), (), s32[]{:S(2)}) async-start(), calls=%async_computation.5 | async-start | bytes 2162688
  250.7 3.0 copy-start
  253.7 2.2 copy-start.7
  253.7 2.3 copy-start.1
  253.7 2.9 copy-start.3
  329.9 3.5 copy-start.2
  329.9 116.9 %collective-permute-start.1 = (f32[64]{0:T(128)S(1)}, f32[64]{0:T(128)S(1)}, u32[]{:S(2)}, u32[]{:S(2)}) collective-permute-start(f32[64]{0:T(128)S(1)} %get-tuple-element.192), channel_id=1, source_target_pairs={{224,0},{0,32},{32,64},{64,96},{96,128},{128,160},{160,192},{192,2... | collective-permute-start | bytes 776 | tf_op jit(solution)/shard_map/ppermute | solution.py:13
  333.4 2.8 copy-start.4
  333.4 2.9 copy-start.5
Sparse Core Ops, SparseCore 0:
  113.8 115.9 reduce-scatter.6
  330.0 115.7 reduce-scatter.8
